TPU v7x, 32 devices: a whole 2x2x4 slice. The times are simulated.
32 devices in a mesh: pre: 2 (over y), dec: 4 (over x, core), rep: 4 (over z).
Axes of the slice: x: 2, y: 2, z: 4, core: 2. Of those that a mesh axis runs over, the one named last changes fastest.
Arguments:
- layer_queries: bfloat16 [2048, 8192], P(('pre', 'rep'), 'dec'), may hold values from -16 to 16
- layer_keys: bfloat16 [2048, 1024], P(('pre', 'rep')), may hold values from -16 to 16
- layer_values: bfloat16 [2048, 1024], P(('pre', 'rep')), may hold values from -6 to 6
- query_bias: float32 [8192], P('dec'), may hold values from -3 to 3
- key_bias: float32 [1024], replicated, may hold values from -3 to 3
- value_bias: float32 [1024], replicated, may hold values from -3 to 3
- positions: int32 [2048], replicated, may hold values from 0 to 2047, each once
- lengths: int32 [32], replicated, may hold values from 1 to 1024, as said below
- replica_of: int32 [32], replicated, may hold values from 0 to 3, as said below
- page_table: int32 [4, 16], replicated, may hold values from 0 to 3, as said below
- prefill_cache: bfloat16 [4, 16, 16, 4, 64, 128], P('rep', 'pre', 'dec'), may hold values from -6 to 6
Outputs:
- context: bfloat16 [2048, 8192], P(('pre', 'rep'), 'dec')
- decode_cache: bfloat16 [4, 4, 8, 16, 4, 64, 128], P('rep', 'dec', None, 'pre')
Inputs may be any that keep to these rules, and one draw needn't show every extreme that they name: `replica_of`: each replica receives exactly 8 requests. `lengths`: the requests of each replica fill exactly 16 blocks of 128 tokens, each request starting a new block; in each replica one request spans exactly 8 full blocks. `page_table`: in each aligned run of 8 blocks of a replica, exactly half of the 4 decode devices appear, each exactly 4 times.
All inputs are finite; a program needn't handle non-finite values.
Results may differ from a plain program's by a relative error of at most 0.0094.
Values may be sent and summed in bfloat16 or wider, within the bound.
No kernel may reach another device: no remote copies, remote signals or barrier semaphores. Data moves between devices by JAX's collectives and lax.ppermute only.
A program may use at most 128 MiB of HBM per device.

v0:
```python
import jax
import jax.numpy as jnp
from jax import lax
from jax.sharding import PartitionSpec as P

HEADS = 64
KVH = 8
HD = 128
BLOCK = 128
rope_base = 1000000.0
masked_score = -1e30


def rotate(values, where_at):
    width = values.shape[-1]
    half_width = width // 2
    freqs = 1.0 / rope_base ** (jnp.arange(half_width, dtype=jnp.float32) * (2.0 / width))
    angles = where_at.astype(jnp.float32)[:, None] * freqs[None, :]
    cosine = jnp.cos(angles)[:, None, :]
    sine = jnp.sin(angles)[:, None, :]
    first = values[..., :half_width]
    second = values[..., half_width:]
    return jnp.concatenate(
        [first * cosine - second * sine, second * cosine + first * sine], axis=-1
    )


def valid_tokens(lengths, replica_of, replica, block_ids):
    member = replica_of == replica
    counts = jnp.where(member, (lengths + (BLOCK - 1)) // BLOCK, 0)
    starts = jnp.cumsum(counts) - counts
    inside = (block_ids[:, None] >= starts[None, :]) & (
        block_ids[:, None] < (starts + counts)[None, :]
    )
    remain = lengths[None, :] - BLOCK * (block_ids[:, None] - starts[None, :])
    return jnp.sum(jnp.where(inside, jnp.clip(remain, 0, BLOCK), 0), axis=1)


def shards(
    layer_queries,
    layer_keys,
    layer_values,
    query_bias,
    key_bias,
    value_bias,
    positions,
    lengths,
    replica_of,
    page_table,
    prefill_cache,
):
    row_count = layer_queries.shape[0]
    head_count = layer_queries.shape[1] // HD
    group_size = HEADS // KVH
    kv_local = max(1, head_count // group_size)
    per_group = head_count // kv_local
    scale = HD ** (-0.5)
    row_start = lax.axis_index(("pre", "rep")) * row_count
    query_pos = lax.dynamic_slice_in_dim(positions, row_start, row_count)
    shifted = layer_queries.astype(jnp.float32).reshape(
        row_count, head_count, HD
    ) + query_bias.reshape(head_count, HD)
    rotated = rotate(shifted, query_pos).astype(jnp.bfloat16)
    query_rows = (
        rotated.reshape(row_count, kv_local, per_group, HD)
        .transpose(1, 2, 0, 3)
        .reshape(kv_local, per_group * row_count, HD)
    )
    query_rowpos = jnp.tile(query_pos, per_group)
    kv_first = lax.axis_index("dec") * head_count // group_size
    bias_keys = lax.dynamic_slice_in_dim(key_bias, kv_first * HD, kv_local * HD).reshape(
        kv_local, HD
    )
    bias_values = lax.dynamic_slice_in_dim(value_bias, kv_first * HD, kv_local * HD).reshape(
        kv_local, HD
    )
    own_keys = lax.dynamic_slice_in_dim(layer_keys, kv_first * HD, kv_local * HD, 1)
    own_values = lax.dynamic_slice_in_dim(layer_values, kv_first * HD, kv_local * HD, 1)
    count = own_keys.shape[0]
    shifted_keys = own_keys.astype(jnp.float32).reshape(count, kv_local, HD) + bias_keys
    keys_rot = rotate(shifted_keys, query_pos).astype(jnp.bfloat16).reshape(count, kv_local * HD)
    values_biased = (
        own_values.astype(jnp.float32).reshape(count, kv_local, HD) + bias_values
    ).astype(jnp.bfloat16)
    local_values = values_biased.reshape(count, kv_local * HD)
    best = jnp.full((kv_local, per_group * row_count), masked_score, jnp.float32)
    piece_keys = lax.all_gather(keys_rot, ("pre", "rep"), axis=0, tiled=True)
    piece_values = lax.all_gather(local_values, ("pre", "rep"), axis=0, tiled=True)
    count = piece_keys.shape[0]
    scores = (
        jnp.einsum(
            "kqd,nkd->kqn",
            query_rows,
            piece_keys.reshape(count, kv_local, HD),
            preferred_element_type=jnp.float32,
        )
        * scale
    )
    allowed = positions[None, None, :] <= query_rowpos[None, :, None]
    scores = jnp.where(allowed, scores, masked_score)
    newest = jnp.maximum(best, jnp.max(scores, axis=2))
    weights = jnp.where(allowed, jnp.exp(scores - newest[:, :, None]), 0.0)
    total = jnp.sum(weights, axis=2)
    added = jnp.einsum(
        "kqn,nkd->kqd",
        weights.astype(jnp.bfloat16),
        piece_values.reshape(count, kv_local, HD),
        preferred_element_type=jnp.float32,
    )
    summed = added
    best, total, summed = (newest, total, summed)
    context = (summed / total[:, :, None]).astype(jnp.bfloat16)
    context = (
        context.reshape(kv_local, per_group, row_count, HD)
        .transpose(2, 0, 1, 3)
        .reshape(row_count, head_count * HD)
    )
    local_cache = prefill_cache[0]
    blk_count = local_cache.shape[0]
    dec_size = lax.axis_size("dec")
    pre_size = lax.axis_size("pre")
    capacity = 2 * blk_count // dec_size
    replica = lax.axis_index("rep")
    run_index = lax.axis_index("pre")
    block_ids = run_index * blk_count + jnp.arange(blk_count, dtype=jnp.int32)
    valid = valid_tokens(lengths, replica_of, replica, block_ids)
    keep = (jnp.arange(BLOCK, dtype=jnp.int32)[None, :] < valid[:, None]).astype(jnp.bfloat16)
    masked = local_cache * keep[:, None, None, None, :]
    page_row = lax.dynamic_index_in_dim(page_table, replica, 0, keepdims=False)
    targets = lax.dynamic_slice_in_dim(page_row, run_index * blk_count, blk_count)
    places = jnp.arange(blk_count, dtype=jnp.int32)
    before_me = (targets[None, :] == targets[:, None]) & (places[None, :] < places[:, None])
    ranks = jnp.sum(before_me, axis=1)
    select = (targets[None, None, :] == jnp.arange(dec_size, dtype=jnp.int32)[:, None, None]) & (
        ranks[None, None, :] == jnp.arange(capacity, dtype=jnp.int32)[None, :, None]
    )
    outgoing = jnp.dot(
        select.reshape(dec_size * capacity, blk_count).astype(jnp.bfloat16),
        masked.reshape(blk_count, -1),
        preferred_element_type=jnp.float32,
    ).astype(jnp.bfloat16)
    outgoing = outgoing.reshape((dec_size, capacity) + local_cache.shape[1:])
    group_halves = 2 * KVH // pre_size
    arrived = lax.all_to_all(
        lax.all_to_all(outgoing, "dec", split_axis=0, concat_axis=2, tiled=True),
        "pre",
        split_axis=2,
        concat_axis=0,
        tiled=True,
    )
    decode_cache = arrived.reshape(
        (1, 1, pre_size * capacity, group_halves) + local_cache.shape[2:]
    )
    return (context, decode_cache)


def solution(mesh):
    placed = (
        P(("pre", "rep"), "dec"),
        P(("pre", "rep"), None),
        P(("pre", "rep"), None),
        P("dec"),
        P(),
        P(),
        P(),
        P(),
        P(),
        P(),
        P("rep", "pre", "dec", None, None, None),
    )
    return jax.shard_map(
        shards,
        mesh=mesh,
        in_specs=placed,
        out_specs=(P(("pre", "rep"), "dec"), P("rep", "dec", None, "pre", None, None, None)),
        check_vma=False,
    )
```

profile of v0, /device:TPU:0, one launch (start us, length us, event | category | flops | bytes accessed | tf_op | source)
XLA Modules:
  0.0 157.9 jit_solution(5007270544340099804)
XLA Ops:
  7.3 1.0 dynamic-slice_convert_fusion
  8.4 0.8 dynamic-slice_bitcast_fusion
  9.3 0.8 fusion.14
  10.0 0.3 multiply_cosine_fusion
  10.4 0.7 pad_maximum_fusion.1
  11.1 0.7 compare_select_fusion
  12.0 0.8 select_reduce_fusion
  13.0 3.0 %broadcast_multiply_fusion = bf16[1,8,4,4,64,128]{5,4,3,2,1,0:T(8,128)(2,1)} fusion(bf16[1,8,4,4,64,128]{5,4,3,2,1,0:T(8,128)(2,1)} %param.21, bf16[8,128]{1,0:T(8,128)(2,1)S(1)} %fusion.10), kind=kLoop, calls=%fused_computation.17 | loop fusion | flops 1048576 | bytes 4196352 | tf_op jit(solution)/shard_map/mul | solution.py:128
  16.0 2.5 %mul.158 = bf16[8,131072]{1,0:T(8,128)(2,1)S(1)} reshape(bf16[1,8,4,4,64,128]{5,4,3,2,1,0:T(8,128)(2,1)} %broadcast_multiply_fusion) | data formatting | bytes 4194304 | tf_op jit(solution)/shard_map/mul | solution.py:128
  18.5 0.8 dynamic-slice_bitcast_fusion.1
  19.5 1.2 fusion.6
  20.7 2.7 %copy.81 = bf16[2,8,1024,128]{3,2,1,0:T(8,128)(2,1)} copy(bf16[2,8,1024,128]{3,1,2,0:T(8,128)(2,1)S(1)} %fusion.6) | data formatting | bytes 8388608
  23.4 5.0 %all-to-all-start = ((bf16[4,4,4,4,64,128]{5,4,3,2,1,0:T(8,128)(2,1)}), bf16[4,4,4,4,64,128]{5,4,3,2,1,0:T(8,128)(2,1)}, u32[]{:S(2)}, u32[]{:S(2)}) async-start(bf16[4,4,4,4,64,128]{5,4,3,2,1,0:T(8,128)(2,1)} %bitcast.51), calls=%async_computation | async-start | bytes 8388608 | tf_op jit(solution)/shard_map/all_to_all | solution.py:145
  28.8 0.8 dynamic_slice.24
  29.6 0.8 add_convert_fusion.1
  30.8 0.4 copy.79
  31.4 0.8 subtract_convert_fusion
  32.1 0.3 copy.60
  32.7 4.1 %broadcast_compare_fusion = pred[2048,2048]{0,1:T(8,128)(4,1)} fusion(s32[2048]{0:T(1024)S(1)} %bitcast.63, s32[2048]{0:T(1024)S(1)} %copy-done.4), kind=kLoop, calls=%fused_computation.8 | loop fusion | flops 4194304 | bytes 4210688 | tf_op jit(solution)/shard_map/le | solution.py:99
  36.9 1.6 pad_maximum_fusion
  38.4 15.1 %all-gather.3.cloned.1.call-done = bf16[2048,256]{0,1:T(8,128)(2,1)} async-done(((bf16[256,256]{0,1:T(8,128)(2,1)}), bf16[2048,256]{0,1:T(8,128)(2,1)}) %all-gather.3.cloned.1.call-update) | async-done | bytes 1048592 | tf_op jit(solution)/shard_map/all_gather | solution.py:87
  53.5 16.9 %fusion = (f32[2,2048]{1,0:T(2,128)S(1)}, f32[2,2048,2048]{1,2,0:T(8,128)}) fusion(pred[2048,2048]{0,1:T(8,128)(4,1)} %broadcast_compare_fusion, bf16[2,2048,128]{2,1,0:T(8,128)(2,1)} %bitcast.58, bf16[2048,2,128]{0,2,1:T(8,128)(2,1)} %bitcast.67), kind=kOutput, calls=%fused_computation.3 | convolution fusion | flops 2172645376 | bytes 39862272 | tf_op jit(solution)/shard_map/kqd,nkd->kqn/dot_general | solution.py:91
  70.4 15.2 %fusion.1 = f32[2,2048]{1,0:T(2,128)S(1)} fusion(f32[2,2048,2048]{1,2,0:T(8,128)} %get-tuple-element.11, f32[2,2048]{1,0:T(2,128)S(1)} %broadcast_maximum_fusion, pred[2048,2048]{0,1:T(8,128)(4,1)S(1)} %copy-done.2), kind=kLoop, calls=%fused_computation.4 | loop fusion | flops 41938944 | bytes 37781504 | tf_op jit(solution)/shard_map/reduce_sum | solution.py:103
  85.7 3.2 %copy.69 = bf16[4,4,4,4,64,128]{5,4,3,2,0,1:T(8,128)(2,1)S(1)} copy(bf16[4,4,4,4,64,128]{5,4,3,2,1,0:T(8,128)(2,1)} %all-to-all-done) | data formatting | bytes 8388608 | tf_op jit(solution)/shard_map/all_to_all | solution.py:145
  88.8 2.9 %copy.70 = bf16[1,4,16,4,64,128]{5,4,3,1,0,2:T(8,128)(2,1)} copy(bf16[1,4,16,4,64,128]{5,4,3,2,1,0:T(8,128)(2,1)S(1)} %bitcast.52) | data formatting | bytes 8388608 | tf_op jit(solution)/shard_map/all_to_all | solution.py:145
  91.8 5.8 %all-to-all-start.1 = ((bf16[1,4,16,4,64,128]{5,4,3,1,0,2:T(8,128)(2,1)}), bf16[1,4,16,4,64,128]{5,4,3,1,0,2:T(8,128)(2,1)}, u32[]{:S(2)}, u32[]{:S(2)}) async-start(bf16[1,4,16,4,64,128]{5,4,3,1,0,2:T(8,128)(2,1)} %copy.70), calls=%async_computation.1 | async-start | bytes 8388608 | tf_op jit(solution)/shard_map/all_to_all | solution.py:144
  97.6 18.3 %divide_convert_fusion = bf16[2,2048,128]{2,1,0:T(8,128)(2,1)S(1)} fusion(bf16[2048,2,128]{0,2,1:T(8,128)(2,1)} %bitcast.68, f32[2,2048,2048]{1,2,0:T(8,128)} %get-tuple-element.11, f32[2,2048]{1,0:T(2,128)S(1)} %broadcast_maximum_fusion, pred[2048,2048]{0,1:T(8,128)(4,1)} %broadcast_compare_fusion, f32[2,2048]{1,0:T(2,128)S(1)} %fusion.1), kind=kOutput, calls=%fused_computation.12 | convolution fusion | flops 2190475264 | bytes 39878656 | tf_op jit(solution)/shard_map/kqn,nkd->kqd/dot_general | solution.py:104
  115.9 0.7 copy.67
  116.6 1.2 copy.83
  117.8 27.1 %all-to-all-done.1 = bf16[1,4,16,4,64,128]{5,4,3,1,0,2:T(8,128)(2,1)} async-done(((bf16[1,4,16,4,64,128]{5,4,3,1,0,2:T(8,128)(2,1)}), bf16[1,4,16,4,64,128]{5,4,3,1,0,2:T(8,128)(2,1)}, u32[]{:S(2)}, u32[]{:S(2)}) %all-to-all-start.1) | async-done | bytes 4194336 | tf_op jit(solution)/shard_map/all_to_all | solution.py:144
  144.9 3.1 %copy.71 = bf16[1,4,16,4,64,128]{5,4,3,2,1,0:T(8,128)(2,1)S(1)} copy(bf16[1,4,16,4,64,128]{5,4,3,1,0,2:T(8,128)(2,1)} %all-to-all-done.1) | data formatting | bytes 8388608 | tf_op jit(solution)/shard_map/all_to_all | solution.py:144
  148.1 3.0 %copy.72 = bf16[2,1,4,8,4,64,128]{6,5,4,3,2,0,1:T(8,128)(2,1)} copy(bf16[2,1,4,8,4,64,128]{6,5,4,3,0,2,1:T(8,128)(2,1)S(1)} %bitcast.53) | data formatting | bytes 8388608 | tf_op jit(solution)/shard_map/all_to_all | solution.py:144
  (41 shorter events, 2.2 us)
Async XLA Ops:
  7.2 21.5 %copy-start = (bf16[256,1024]{1,0:T(8,128)(2,1)S(1)}, bf16[256,1024]{1,0:T(8,128)(2,1)}, u32[]{:S(2)}) copy-start(bf16[256,1024]{1,0:T(8,128)(2,1)} %param.13) | copy-start | bytes 1572868
  7.2 46.3 %all-gather.3.cloned.1.call-start = ((), (), s32[]{:S(2)}) async-start(), calls=%async_computation.2 | async-start | bytes 1179648 | tf_op jit(solution)/shard_map/all_gather | solution.py:87
  23.4 7.1 %copy-start.3 = (bf16[256,2048]{1,0:T(8,128)(2,1)S(1)}, bf16[256,2048]{1,0:T(8,128)(2,1)}, u32[]{:S(2)}) copy-start(bf16[256,2048]{1,0:T(8,128)(2,1)} %param.11) | copy-start | bytes 3145732
  23.4 62.2 %all-to-all-start = ((bf16[4,4,4,4,64,128]{5,4,3,2,1,0:T(8,128)(2,1)}), bf16[4,4,4,4,64,128]{5,4,3,2,1,0:T(8,128)(2,1)}, u32[]{:S(2)}, u32[]{:S(2)}) async-start(bf16[4,4,4,4,64,128]{5,4,3,2,1,0:T(8,128)(2,1)} %bitcast.51), calls=%async_computation | async-start | bytes 8388608 | tf_op jit(solution)/shard_map/all_to_all | solution.py:145
  28.4 69.2 %all-gather.5.cloned.1.call-start = ((), (), s32[]{:S(2)}) async-start(), calls=%async_computation.3 | async-start | bytes 1179648 | tf_op jit(solution)/shard_map/all_gather | solution.py:88
  28.7 2.5 %copy-start.5 = (f32[2048]{0:T(1024)S(1)}, f32[2048]{0:T(1024)}, u32[]{:S(2)}) copy-start(f32[2048]{0:T(1024)} %param.14) | copy-start | bytes 24580
  31.4 1.4 copy-start.4
  53.5 16.9 %copy-start.2 = (pred[2048,2048]{0,1:T(8,128)(4,1)S(1)}, pred[2048,2048]{0,1:T(8,128)(4,1)}, u32[]{:S(2)}) copy-start(pred[2048,2048]{0,1:T(8,128)(4,1)} %broadcast_compare_fusion) | copy-start | bytes 12582916
  91.8 53.2 %all-to-all-start.1 = ((bf16[1,4,16,4,64,128]{5,4,3,1,0,2:T(8,128)(2,1)}), bf16[1,4,16,4,64,128]{5,4,3,1,0,2:T(8,128)(2,1)}, u32[]{:S(2)}, u32[]{:S(2)}) async-start(bf16[1,4,16,4,64,128]{5,4,3,1,0,2:T(8,128)(2,1)} %copy.70), calls=%async_computation.1 | async-start | bytes 8388608 | tf_op jit(solution)/shard_map/all_to_all | solution.py:144
  148.1 3.0 %copy-start.1 = (bf16[256,1024]{1,0:T(8,128)(2,1)S(1)}, bf16[256,1024]{1,0:T(8,128)(2,1)}, u32[]{:S(2)}) copy-start(bf16[256,1024]{1,0:T(8,128)(2,1)} %param.13) | copy-start | bytes 1572868
Sparse Core Ops, SparseCore 0:
  11.2 42.2 all-gather.2
  55.5 38.4 all-gather.4
where the time goes:
time: 159 us; the launch traced here: 158 us
  waiting for transfers between devices  42.3 us (27%)
  matrix products  36.4 us (23%)
  other arithmetic  30.7 us (19%)
  local copies, waits for them, and re-layouts  23.1 us (15%)
  between operations  14.4 us (9%)
  starting transfers between devices  11.1 us (7%)
    all_to_all x1, waiting for transfers between devices, shards(): lax.all_to_all(lax.all_to_all(outgoing, 'dec', split_axis=0, concat_axis=...  27.1 us
    dot_general x1, matrix products, shards(): jnp.einsum('kqn,nkd->kqd', weights.astype(jnp.bfloat16), piece_values.res...  18.3 us
    dot_general x1, matrix products, shards(): jnp.einsum('kqd,nkd->kqn', query_rows, piece_keys.reshape(count, kv_local...  16.9 us
    reduce_sum x1, other arithmetic, shards(): total = jnp.sum(weights, axis=2)  15.2 us
    all_gather x1, waiting for transfers between devices, shards(): piece_keys = lax.all_gather(keys_rot, ('pre', 'rep'), axis=0, tiled=True)  15.1 us
    all_to_all x2, local copies, waits for them, and re-layouts, shards(): lax.all_to_all(lax.all_to_all(outgoing, 'dec', split_axis=0, concat_axis=...  6.13 us
    all_to_all x2, local copies, waits for them, and re-layouts, shards(): lax.all_to_all(outgoing, 'dec', split_axis=0, concat_axis=2, tiled=True)  6.08 us
    all_to_all x1, starting transfers between devices, shards(): lax.all_to_all(lax.all_to_all(outgoing, 'dec', split_axis=0, concat_axis=...  5.82 us
  transfers between devices with their start and end apart: 4, of which 2 were waited for; matrix products, arithmetic and copies ran while one was open for 51% of the time, Pallas kernels for 0%

commit v1 on v0

--- a/solution.py
+++ b/solution.py
@@ -9,6 +9,25 @@
 BLOCK = 128
 rope_base = 1000000.0
 masked_score = -1e30
+
+
+def gather_around(value, axis, dim):
+    count, mine, rows = (lax.axis_size(axis), lax.axis_index(axis), value.shape[dim])
+    ahead = [(i, (i + 1) % count) for i in range(count)]
+    left = [(i, (i - 1) % count) for i in range(count)]
+    out = jnp.zeros((*value.shape[:dim], count * rows, *value.shape[dim + 1 :]), value.dtype)
+    out = lax.dynamic_update_slice_in_dim(out, value, mine * rows, axis=dim)
+    from_left = from_right = value
+    half = count // 2
+    for lap in range(1, half + 1):
+        from_left = lax.ppermute(from_left, axis, ahead)
+        out = lax.dynamic_update_slice_in_dim(out, from_left, (mine - lap) % count * rows, axis=dim)
+        if lap < count - half:
+            from_right = lax.ppermute(from_right, axis, left)
+            out = lax.dynamic_update_slice_in_dim(
+                out, from_right, (mine + lap) % count * rows, axis=dim
+            )
+    return out
 
 
 def rotate(values, where_at):
@@ -84,7 +103,7 @@
     ).astype(jnp.bfloat16)
     local_values = values_biased.reshape(count, kv_local * HD)
     best = jnp.full((kv_local, per_group * row_count), masked_score, jnp.float32)
-    piece_keys = lax.all_gather(keys_rot, ("pre", "rep"), axis=0, tiled=True)
+    piece_keys = gather_around(keys_rot, ("pre", "rep"), 0)
     piece_values = lax.all_gather(local_values, ("pre", "rep"), axis=0, tiled=True)
     count = piece_keys.shape[0]
     scores = (

time: 159 us -> 176 us (1.11)
  starting transfers between devices: 11.1 us -> 24.6 us
  local copies, waits for them, and re-layouts: 23.1 us -> 31.6 us
  waiting for transfers between devices: 42.3 us -> 38.5 us
    all_gather x1 -> x0, waiting for transfers between devices: 15.1 us -> none  [shards(): piece_keys = lax.all_gather(keys_rot, ('pre', 'rep'), axis=0, tiled=True)]
    ppermute x0 -> x7, waiting for transfers between devices: none -> 15.1 us  [the longest x4 13.3 us: gather_around(): from_left = lax.ppermute(from_left, axis, ahead)]
    ppermute x0 -> x7, starting transfers between devices: none -> 13.8 us  [the longest x3 10.7 us: gather_around(): from_right = lax.ppermute(from_right, axis, left)]
    dynamic_update_slice x0 -> x8, local copies, waits for them, and re-layouts: none -> 5.46 us  [the longest x4 2.71 us: gather_around(): lax.dynamic_update_slice_in_dim(out, from_left, (mine - lap) % count * ro...]
    all_to_all x1, waiting for transfers between devices: 27.1 us -> 23.4 us  [shards(): lax.all_to_all(lax.all_to_all(outgoing, 'dec', split_axis=0, concat_axis=...]
    another operation x3, local copies, waits for them, and re-layouts: 0.63 us -> 2.57 us
    unnamed x18 -> x20, local copies, waits for them, and re-layouts: 4.5 us -> 4.5 us
  transfers between devices with their start and end apart: 4 -> 10, of which waited for: 2 -> 5; matrix products, arithmetic and copies ran while one was open for 51% -> 50% of each run, Pallas kernels for 0% -> 0%
where the time goes in v1:
time: 176 us; the launch traced here: 175 us
  waiting for transfers between devices  38.5 us (22%)
  matrix products  35.5 us (20%)
  local copies, waits for them, and re-layouts  31.6 us (18%)
  other arithmetic  30.2 us (17%)
  starting transfers between devices  24.6 us (14%)
  between operations  14.5 us (8%)
    all_to_all x1, waiting for transfers between devices, shards(): lax.all_to_all(lax.all_to_all(outgoing, 'dec', split_axis=0, concat_axis=...  23.4 us
    dot_general x1, matrix products, shards(): jnp.einsum('kqn,nkd->kqd', weights.astype(jnp.bfloat16), piece_values.res...  18.3 us
    dot_general x1, matrix products, shards(): jnp.einsum('kqd,nkd->kqn', query_rows, piece_keys.reshape(count, kv_local...  16 us
    reduce_sum x1, other arithmetic, shards(): total = jnp.sum(weights, axis=2)  15.1 us
    ppermute x4, waiting for transfers between devices, gather_around(): from_left = lax.ppermute(from_left, axis, ahead)  13.3 us
    ppermute x3, starting transfers between devices, gather_around(): from_right = lax.ppermute(from_right, axis, left)  10.7 us
    all_to_all x2, local copies, waits for them, and re-layouts, shards(): lax.all_to_all(lax.all_to_all(outgoing, 'dec', split_axis=0, concat_axis=...  6.13 us
    all_to_all x2, local copies, waits for them, and re-layouts, shards(): lax.all_to_all(outgoing, 'dec', split_axis=0, concat_axis=2, tiled=True)  6.06 us
  transfers between devices with their start and end apart: 10, of which 5 were waited for; matrix products, arithmetic and copies ran while one was open for 50% of the time, Pallas kernels for 0%

profile of v1, /device:TPU:0, one launch (start us, length us, event | category | flops | bytes accessed | tf_op | source)
XLA Modules:
  0.0 174.9 jit_solution(4792872474891235849)
XLA Ops:
  7.3 1.1 dynamic-slice_convert_fusion
  9.4 0.8 fusion.14
  10.5 3.1 %collective-permute-start = (bf16[256,256]{0,1:T(8,128)(2,1)S(1)}, bf16[256,256]{0,1:T(8,128)(2,1)S(1)}, u32[]{:S(2)}, u32[]{:S(2)}) collective-permute-start(bf16[256,256]{0,1:T(8,128)(2,1)S(1)} %bitcast.62), channel_id=1, source_target_pairs={{0,1},{1,2},{2,3},{3,16},{16,17},{17,18},{18,19},{19,0},{4,5},{5,6... | collective-permute-start | bytes 393224 | tf_op jit(solution)/shard_map/ppermute | solution.py:23
  13.6 3.0 %collective-permute-start.1 = (bf16[256,256]{0,1:T(8,128)(2,1)S(1)}, bf16[256,256]{0,1:T(8,128)(2,1)S(1)}, u32[]{:S(2)}, u32[]{:S(2)}) collective-permute-start(bf16[256,256]{0,1:T(8,128)(2,1)S(1)} %bitcast.63), channel_id=1, source_target_pairs={{0,19},{1,0},{2,1},{3,2},{16,3},{17,16},{18,17},{19,18},{4,23},{5,... | collective-permute-start | bytes 393224 | tf_op jit(solution)/shard_map/ppermute | solution.py:26
  20.2 0.8 select_reduce_fusion
  21.2 1.5 broadcast_multiply_fusion
  22.6 2.5 %mul.188 = bf16[8,131072]{1,0:T(8,128)(2,1)S(1)} reshape(bf16[1,8,4,4,64,128]{5,4,3,2,1,0:T(8,128)(2,1)} %broadcast_multiply_fusion) | data formatting | bytes 4194304 | tf_op jit(solution)/shard_map/mul | solution.py:147
  25.1 1.2 fusion.6
  26.4 2.7 %copy.81 = bf16[2,8,1024,128]{3,2,1,0:T(8,128)(2,1)} copy(bf16[2,8,1024,128]{3,1,2,0:T(8,128)(2,1)S(1)} %fusion.6) | data formatting | bytes 8388608
  29.1 5.0 %all-to-all-start = ((bf16[4,4,4,4,64,128]{5,4,3,2,1,0:T(8,128)(2,1)}), bf16[4,4,4,4,64,128]{5,4,3,2,1,0:T(8,128)(2,1)}, u32[]{:S(2)}, u32[]{:S(2)}) async-start(bf16[4,4,4,4,64,128]{5,4,3,2,1,0:T(8,128)(2,1)} %bitcast.51), calls=%async_computation | async-start | bytes 8388608 | tf_op jit(solution)/shard_map/all_to_all | solution.py:164
  34.4 1.1 broadcast_in_dim.26
  37.0 0.8 subtract_convert_fusion
  37.8 1.2 copy.60
  39.0 1.2 copy.61
  40.3 4.1 %broadcast_compare_fusion = pred[2048,2048]{0,1:T(8,128)(4,1)} fusion(s32[2048]{0:T(1024)S(1)} %bitcast.65, s32[2048]{0:T(1024)S(1)} %copy-done.5), kind=kLoop, calls=%fused_computation.8 | loop fusion | flops 4194304 | bytes 4210688 | tf_op jit(solution)/shard_map/le | solution.py:118
  44.4 3.3 %pad_maximum_fusion = bf16[256,2,8,128]{3,0,2,1:T(8,128)(2,1)} fusion(bf16[256,2,8,64]{3,0,2,1:T(8,128)(2,1)} %bitcast.55, bf16[256,2,8,64]{3,0,2,1:T(8,128)(2,1)} %bitcast.54), kind=kLoop, calls=%fused_computation.16 | loop fusion | flops 2097152 | bytes 2097152 | tf_op jit(solution)/shard_map/concatenate | solution.py:42
  47.7 4.7 %collective-permute-start.3 = (bf16[256,256]{0,1:T(8,128)(2,1)S(1)}, bf16[256,256]{0,1:T(8,128)(2,1)S(1)}, u32[]{:S(2)}, u32[]{:S(2)}) collective-permute-start(bf16[256,256]{0,1:T(8,128)(2,1)S(1)} %collective-permute-done.1), channel_id=1, source_target_pairs={{0,19},{1,0},{2,1},{3,2},{16,3},{17,16},{18,17},{19,18},{4,23},{5,... | collective-permute-start | bytes 393224 | tf_op jit(solution)/shard_map/ppermute | solution.py:26
  53.8 4.5 %collective-permute-done.2 = bf16[256,256]{0,1:T(8,128)(2,1)S(1)} collective-permute-done((bf16[256,256]{0,1:T(8,128)(2,1)S(1)}, bf16[256,256]{0,1:T(8,128)(2,1)S(1)}, u32[]{:S(2)}, u32[]{:S(2)}) %collective-permute-start.2) | collective-permute-done | bytes 131104 | tf_op jit(solution)/shard_map/ppermute | solution.py:23
  58.2 1.8 %collective-permute-done.3 = bf16[256,256]{0,1:T(8,128)(2,1)S(1)} collective-permute-done((bf16[256,256]{0,1:T(8,128)(2,1)S(1)}, bf16[256,256]{0,1:T(8,128)(2,1)S(1)}, u32[]{:S(2)}, u32[]{:S(2)}) %collective-permute-start.3) | collective-permute-done | bytes 131104 | tf_op jit(solution)/shard_map/ppermute | solution.py:26
  60.0 2.9 %collective-permute-start.5 = (bf16[256,256]{0,1:T(8,128)(2,1)S(1)}, bf16[256,256]{0,1:T(8,128)(2,1)S(1)}, u32[]{:S(2)}, u32[]{:S(2)}) collective-permute-start(bf16[256,256]{0,1:T(8,128)(2,1)S(1)} %collective-permute-done.3), channel_id=1, source_target_pairs={{0,19},{1,0},{2,1},{3,2},{16,3},{17,16},{18,17},{19,18},{4,23},{5,... | collective-permute-start | bytes 393224 | tf_op jit(solution)/shard_map/ppermute | solution.py:26
  64.3 2.5 %collective-permute-done.4 = bf16[256,256]{0,1:T(8,128)(2,1)S(1)} collective-permute-done((bf16[256,256]{0,1:T(8,128)(2,1)S(1)}, bf16[256,256]{0,1:T(8,128)(2,1)S(1)}, u32[]{:S(2)}, u32[]{:S(2)}) %collective-permute-start.4) | collective-permute-done | bytes 131104 | tf_op jit(solution)/shard_map/ppermute | solution.py:23
  68.3 6.3 %collective-permute-done.6 = bf16[256,256]{0,1:T(8,128)(2,1)S(1)} collective-permute-done((bf16[256,256]{0,1:T(8,128)(2,1)S(1)}, bf16[256,256]{0,1:T(8,128)(2,1)S(1)}, u32[]{:S(2)}, u32[]{:S(2)}) %collective-permute-start.6) | collective-permute-done | bytes 131104 | tf_op jit(solution)/shard_map/ppermute | solution.py:23
  75.2 16.0 %fusion = (f32[2,2048]{1,0:T(2,128)S(1)}, f32[2,2048,2048]{1,2,0:T(8,128)}) fusion(pred[2048,2048]{0,1:T(8,128)(4,1)S(1)} %copy-done.2, bf16[2,2048,128]{2,1,0:T(8,128)(2,1)} %bitcast.58, bf16[2048,2,128]{0,2,1:T(8,128)(2,1)} %bitcast.8), kind=kOutput, calls=%fused_computation.3 | convolution fusion | flops 2172645376 | bytes 39862272 | tf_op jit(solution)/shard_map/kqd,nkd->kqn/dot_general | solution.py:110
  91.2 15.1 %fusion.1 = f32[2,2048]{1,0:T(2,128)S(1)} fusion(f32[2,2048,2048]{1,2,0:T(8,128)} %get-tuple-element.11, f32[2,2048]{1,0:T(2,128)S(1)} %broadcast_maximum_fusion, pred[2048,2048]{0,1:T(8,128)(4,1)S(1)} %copy-done.2), kind=kLoop, calls=%fused_computation.4 | loop fusion | flops 41938944 | bytes 37781504 | tf_op jit(solution)/shard_map/reduce_sum | solution.py:122
  106.3 3.1 %copy.69 = bf16[4,4,4,4,64,128]{5,4,3,2,0,1:T(8,128)(2,1)S(1)} copy(bf16[4,4,4,4,64,128]{5,4,3,2,1,0:T(8,128)(2,1)} %all-to-all-done) | data formatting | bytes 8388608 | tf_op jit(solution)/shard_map/all_to_all | solution.py:164
  109.5 2.9 %copy.70 = bf16[1,4,16,4,64,128]{5,4,3,1,0,2:T(8,128)(2,1)} copy(bf16[1,4,16,4,64,128]{5,4,3,2,1,0:T(8,128)(2,1)S(1)} %bitcast.52) | data formatting | bytes 8388608 | tf_op jit(solution)/shard_map/all_to_all | solution.py:164
  112.4 5.8 %all-to-all-start.1 = ((bf16[1,4,16,4,64,128]{5,4,3,1,0,2:T(8,128)(2,1)}), bf16[1,4,16,4,64,128]{5,4,3,1,0,2:T(8,128)(2,1)}, u32[]{:S(2)}, u32[]{:S(2)}) async-start(bf16[1,4,16,4,64,128]{5,4,3,1,0,2:T(8,128)(2,1)} %copy.70), calls=%async_computation.1 | async-start | bytes 8388608 | tf_op jit(solution)/shard_map/all_to_all | solution.py:163
  118.3 18.3 %divide_convert_fusion = bf16[2,2048,128]{2,1,0:T(8,128)(2,1)S(1)} fusion(f32[2,2048]{1,0:T(2,128)S(1)} %fusion.1, bf16[2048,2,128]{0,2,1:T(8,128)(2,1)} %bitcast.69, f32[2,2048,2048]{1,2,0:T(8,128)} %get-tuple-element.11, f32[2,2048]{1,0:T(2,128)S(1)} %broadcast_maximum_fusion, pred[2048,2048]{0,1:T(8,128)(4,1)} %broadcast_compare_fusion), kind=kOutput, calls=%fused_computation.12 | convolution fusion | flops 2190475264 | bytes 39878656 | tf_op jit(solution)/shard_map/kqn,nkd->kqd/dot_general | solution.py:123
  137.2 1.2 copy.83
  138.5 23.4 %all-to-all-done.1 = bf16[1,4,16,4,64,128]{5,4,3,1,0,2:T(8,128)(2,1)} async-done(((bf16[1,4,16,4,64,128]{5,4,3,1,0,2:T(8,128)(2,1)}), bf16[1,4,16,4,64,128]{5,4,3,1,0,2:T(8,128)(2,1)}, u32[]{:S(2)}, u32[]{:S(2)}) %all-to-all-start.1) | async-done | bytes 4194336 | tf_op jit(solution)/shard_map/all_to_all | solution.py:163
  161.9 3.1 %copy.71 = bf16[1,4,16,4,64,128]{5,4,3,2,1,0:T(8,128)(2,1)S(1)} copy(bf16[1,4,16,4,64,128]{5,4,3,1,0,2:T(8,128)(2,1)} %all-to-all-done.1) | data formatting | bytes 8388608 | tf_op jit(solution)/shard_map/all_to_all | solution.py:163
  165.1 3.0 %copy.72 = bf16[2,1,4,8,4,64,128]{6,5,4,3,2,0,1:T(8,128)(2,1)} copy(bf16[2,1,4,8,4,64,128]{6,5,4,3,0,2,1:T(8,128)(2,1)S(1)} %bitcast.53) | data formatting | bytes 8388608 | tf_op jit(solution)/shard_map/all_to_all | solution.py:163
  (63 shorter events, 12.2 us)
Async XLA Ops:
  7.2 9.5 %copy-start = (bf16[256,1024]{1,0:T(8,128)(2,1)S(1)}, bf16[256,1024]{1,0:T(8,128)(2,1)}, u32[]{:S(2)}) copy-start(bf16[256,1024]{1,0:T(8,128)(2,1)} %param.13) | copy-start | bytes 1572868
  7.2 14.0 %copy-start.3 = (bf16[1,8,4,4,64,128]{5,4,3,2,1,0:T(8,128)(2,1)S(1)}, bf16[1,8,4,4,64,128]{5,4,3,2,1,0:T(8,128)(2,1)}, u32[]{:S(2)}) copy-start(bf16[1,8,4,4,64,128]{5,4,3,2,1,0:T(8,128)(2,1)} %param.21) | copy-start | bytes 6291460
  7.2 111.1 %all-gather.2.cloned.1.call-start = ((), (), s32[]{:S(2)}) async-start(), calls=%async_computation.2 | async-start | bytes 1179648 | tf_op jit(solution)/shard_map/all_gather | solution.py:107
  10.5 37.2 %collective-permute-start = (bf16[256,256]{0,1:T(8,128)(2,1)S(1)}, bf16[256,256]{0,1:T(8,128)(2,1)S(1)}, u32[]{:S(2)}, u32[]{:S(2)}) collective-permute-start(bf16[256,256]{0,1:T(8,128)(2,1)S(1)} %bitcast.62), channel_id=1, source_target_pairs={{0,1},{1,2},{2,3},{3,16},{16,17},{17,18},{18,19},{19,0},{4,5},{5,6... | collective-permute-start | bytes 393224 | tf_op jit(solution)/shard_map/ppermute | solution.py:23
  13.6 34.1 %collective-permute-start.1 = (bf16[256,256]{0,1:T(8,128)(2,1)S(1)}, bf16[256,256]{0,1:T(8,128)(2,1)S(1)}, u32[]{:S(2)}, u32[]{:S(2)}) collective-permute-start(bf16[256,256]{0,1:T(8,128)(2,1)S(1)} %bitcast.63), channel_id=1, source_target_pairs={{0,19},{1,0},{2,1},{3,2},{16,3},{17,16},{18,17},{19,18},{4,23},{5,... | collective-permute-start | bytes 393224 | tf_op jit(solution)/shard_map/ppermute | solution.py:26
  29.1 7.1 %copy-start.4 = (bf16[256,2048]{1,0:T(8,128)(2,1)S(1)}, bf16[256,2048]{1,0:T(8,128)(2,1)}, u32[]{:S(2)}) copy-start(bf16[256,2048]{1,0:T(8,128)(2,1)} %param.11) | copy-start | bytes 3145732
  29.1 77.2 %all-to-all-start = ((bf16[4,4,4,4,64,128]{5,4,3,2,1,0:T(8,128)(2,1)}), bf16[4,4,4,4,64,128]{5,4,3,2,1,0:T(8,128)(2,1)}, u32[]{:S(2)}, u32[]{:S(2)}) async-start(bf16[4,4,4,4,64,128]{5,4,3,2,1,0:T(8,128)(2,1)} %bitcast.51), calls=%async_computation | async-start | bytes 8388608 | tf_op jit(solution)/shard_map/all_to_all | solution.py:164
  34.4 2.4 %copy-start.6 = (f32[2048]{0:T(1024)S(1)}, f32[2048]{0:T(1024)}, u32[]{:S(2)}) copy-start(f32[2048]{0:T(1024)} %param.14) | copy-start | bytes 24580
  37.0 3.3 %copy-start.5 = (s32[2048]{0:T(1024)S(1)}, s32[2048]{0:T(1024)}, u32[]{:S(2)}) copy-start(s32[2048]{0:T(1024)} %param.17) | copy-start | bytes 24580
  44.4 30.8 %copy-start.2 = (pred[2048,2048]{0,1:T(8,128)(4,1)S(1)}, pred[2048,2048]{0,1:T(8,128)(4,1)}, u32[]{:S(2)}) copy-start(pred[2048,2048]{0,1:T(8,128)(4,1)} %broadcast_compare_fusion) | copy-start | bytes 12582916
  47.7 10.5 %collective-permute-start.2 = (bf16[256,256]{0,1:T(8,128)(2,1)S(1)}, bf16[256,256]{0,1:T(8,128)(2,1)S(1)}, u32[]{:S(2)}, u32[]{:S(2)}) collective-permute-start(bf16[256,256]{0,1:T(8,128)(2,1)S(1)} %collective-permute-done), channel_id=1, source_target_pairs={{0,1},{1,2},{2,3},{3,16},{16,17},{17,18},{18,19},{19,0},{4,5},{5,6... | collective-permute-start | bytes 393224 | tf_op jit(solution)/shard_map/ppermute | solution.py:23
  47.7 12.3 %collective-permute-start.3 = (bf16[256,256]{0,1:T(8,128)(2,1)S(1)}, bf16[256,256]{0,1:T(8,128)(2,1)S(1)}, u32[]{:S(2)}, u32[]{:S(2)}) collective-permute-start(bf16[256,256]{0,1:T(8,128)(2,1)S(1)} %collective-permute-done.1), channel_id=1, source_target_pairs={{0,19},{1,0},{2,1},{3,2},{16,3},{17,16},{18,17},{19,18},{4,23},{5,... | collective-permute-start | bytes 393224 | tf_op jit(solution)/shard_map/ppermute | solution.py:26
  58.2 8.6 %collective-permute-start.4 = (bf16[256,256]{0,1:T(8,128)(2,1)S(1)}, bf16[256,256]{0,1:T(8,128)(2,1)S(1)}, u32[]{:S(2)}, u32[]{:S(2)}) collective-permute-start(bf16[256,256]{0,1:T(8,128)(2,1)S(1)} %collective-permute-done.2), channel_id=1, source_target_pairs={{0,1},{1,2},{2,3},{3,16},{16,17},{17,18},{18,19},{19,0},{4,5},{5,6... | collective-permute-start | bytes 393224 | tf_op jit(solution)/shard_map/ppermute | solution.py:23
  60.0 7.5 %collective-permute-start.5 = (bf16[256,256]{0,1:T(8,128)(2,1)S(1)}, bf16[256,256]{0,1:T(8,128)(2,1)S(1)}, u32[]{:S(2)}, u32[]{:S(2)}) collective-permute-start(bf16[256,256]{0,1:T(8,128)(2,1)S(1)} %collective-permute-done.3), channel_id=1, source_target_pairs={{0,19},{1,0},{2,1},{3,2},{16,3},{17,16},{18,17},{19,18},{4,23},{5,... | collective-permute-start | bytes 393224 | tf_op jit(solution)/shard_map/ppermute | solution.py:26
  66.9 7.7 %collective-permute-start.6 = (bf16[256,256]{0,1:T(8,128)(2,1)S(1)}, bf16[256,256]{0,1:T(8,128)(2,1)S(1)}, u32[]{:S(2)}, u32[]{:S(2)}) collective-permute-start(bf16[256,256]{0,1:T(8,128)(2,1)S(1)} %collective-permute-done.4), channel_id=1, source_target_pairs={{0,1},{1,2},{2,3},{3,16},{16,17},{17,18},{18,19},{19,0},{4,5},{5,6... | collective-permute-start | bytes 393224 | tf_op jit(solution)/shard_map/ppermute | solution.py:23
  112.4 49.5 %all-to-all-start.1 = ((bf16[1,4,16,4,64,128]{5,4,3,1,0,2:T(8,128)(2,1)}), bf16[1,4,16,4,64,128]{5,4,3,1,0,2:T(8,128)(2,1)}, u32[]{:S(2)}, u32[]{:S(2)}) async-start(bf16[1,4,16,4,64,128]{5,4,3,1,0,2:T(8,128)(2,1)} %copy.70), calls=%async_computation.1 | async-start | bytes 8388608 | tf_op jit(solution)/shard_map/all_to_all | solution.py:163
  165.0 3.0 %copy-start.1 = (bf16[256,1024]{1,0:T(8,128)(2,1)S(1)}, bf16[256,1024]{1,0:T(8,128)(2,1)}, u32[]{:S(2)}) copy-start(bf16[256,1024]{1,0:T(8,128)(2,1)} %param.13) | copy-start | bytes 1572868
Sparse Core Ops, SparseCore 0:
  18.4 42.7 all-gather.1
